TPU v7x, 32 devices: a whole 2x2x4 slice. The times are simulated.
32 devices in a mesh: scan: 2 (over y), ang: 4 (over z), row: 4 (over x, core).
Axes of the slice: x: 2, y: 2, z: 4, core: 2. Of those that a mesh axis runs over, the one named last changes fastest.
Arguments:
- raw_frames: bfloat16 [96, 128, 2560], P(('scan', 'ang'), 'row'), parts along dimension 0, may hold values from 0.099609375 to 1.5
- dark_field: bfloat16 [128, 2560], P('row'), may hold values from 0 to 0.079589844
- flat_field: bfloat16 [128, 2560], P('row'), may hold values from 0.796875 to 1.1953125
- kernel_taps: float32 [31], replicated, may hold values from 0.1 to 0.4
- partner: int32 [48], P('scan'), parts along dimension 0, may hold values from 24 to 47, as said below
- shifts: int32 [256], replicated, may hold values from -256 to 255, as said below
Outputs:
- sinograms: bfloat16 [96, 128, 2560], P('scan', ('ang', 'row')), parts along dimension 0
- correlation: float32 [256, 256], P(('scan', 'ang', 'row')), parts along dimension 0
There are 2 independent parts, one for each index of `scan`. A program takes and returns all parts, laid end to end along the dimension named above; an argument that names none is the same for every part. Nothing has to cross between parts.
Inputs may be any that keep to these rules, and one draw needn't show every extreme that they name: partner[i] - i - 24 is -1, 0 or 1 for every i; partner[0] = 24 and partner[23] = 47. shifts[0] = -256 and shifts[255] = 255; values may repeat.
All inputs are finite; a program needn't handle non-finite values.
Results may differ from a plain program's by a relative error of at most 0.012.
The roundings to bfloat16 on the way count: a program that leaves them out, or rounds other values in their place, can miss the bound.
Values may be sent and summed in bfloat16 or wider, within the bound.
A program may use at most 128 MiB of HBM per device.

v0:
```python
import math

import jax
import jax.numpy as jnp
from jax import lax
from jax.sharding import PartitionSpec as P

SPAN = 256


def padded_2(cells, sides, width):
    for axis, dim in sides:
        count = lax.axis_size(axis)
        ends = count - 1
        head = lax.slice_in_dim(cells, 0, width, axis=dim)
        tail = lax.slice_in_dim(cells, cells.shape[dim] - width, cells.shape[dim], axis=dim)
        cells = jnp.concatenate(
            [
                lax.ppermute(tail, axis, [(i, (i + 1) % count) for i in range(ends)]),
                cells,
                lax.ppermute(head, axis, [((i + 1) % count, i) for i in range(ends)]),
            ],
            axis=dim,
        )
    return cells


def absorb(raw_frames, dark_field, flat_field):
    counts = raw_frames.astype(jnp.float32)
    darkness = dark_field.astype(jnp.float32)
    brightness = flat_field.astype(jnp.float32)
    return -jnp.log((counts - darkness) / (brightness - darkness))


def column_pass(signal, kernel_taps):
    margin = kernel_taps.shape[0] // 2
    col_count = signal.shape[-1]
    padding = [(0, 0)] * (signal.ndim - 1) + [(margin, margin)]
    padded = jnp.pad(signal, padding)
    summed = kernel_taps[0] * padded[..., 0:col_count]
    for tap_index in range(1, kernel_taps.shape[0]):
        summed = summed + kernel_taps[tap_index] * padded[..., tap_index : tap_index + col_count]
    return summed


def row_pass(extended, kernel_taps, row_count, row_axis):
    summed = kernel_taps[0] * lax.slice_in_dim(extended, 0, row_count, axis=row_axis)
    for tap_index in range(1, kernel_taps.shape[0]):
        summed = summed + kernel_taps[tap_index] * lax.slice_in_dim(
            extended, tap_index, tap_index + row_count, axis=row_axis
        )
    return summed


def center_lines(lowpassed):
    return (lowpassed - jnp.mean(lowpassed, axis=-1, keepdims=True)).astype(jnp.bfloat16)


def ramp_matrix(col_count):
    distance = lax.iota(jnp.int32, col_count)[:, None] - lax.iota(jnp.int32, col_count)[None, :]
    spacing = distance.astype(jnp.float32)
    odd_distance = distance % 2 != 0
    falloff = -4.0 / (math.pi * math.pi * jnp.maximum(spacing * spacing, 1.0))
    kernel = jnp.where(distance == 0, 1.0, jnp.where(odd_distance, falloff, 0.0))
    return kernel.astype(jnp.bfloat16)


def apply_ramp(lines, ramp_kernel):
    col_count = lines.shape[-1]
    ramped = jnp.dot(lines.reshape(-1, col_count), ramp_kernel, preferred_element_type=jnp.float32)
    return ramped.astype(jnp.bfloat16).reshape(lines.shape)


def shards(raw_frames, dark_field, flat_field, kernel_taps, partner, shifts):
    planes, row_count, col_count = raw_frames.shape
    margin = kernel_taps.shape[0] // 2
    smooth = column_pass(absorb(raw_frames, dark_field[None], flat_field[None]), kernel_taps)
    extended = padded_2(smooth, (("row", 1),), margin)
    lowpassed = row_pass(extended, kernel_taps, row_count, 1)
    centered = center_lines(lowpassed)
    ang_count = lax.axis_size("ang")
    row_devices = lax.axis_size("row")
    upper_count = ang_count // row_devices
    row_share = row_count // ang_count
    shaped = centered.reshape(planes, upper_count, row_devices, row_share, col_count)
    ramp_kernel = ramp_matrix(col_count)
    across = lax.all_to_all(shaped, "row", split_axis=2, concat_axis=1, tiled=True)
    gathered = lax.all_to_all(across, "ang", split_axis=1, concat_axis=0, tiled=True)
    sinogram = gathered.reshape(-1, row_share, col_count)
    filtered = apply_ramp(sinogram, ramp_kernel)
    half_count = sinogram.shape[0] // 2
    leading = sinogram[:half_count]
    offset = partner - lax.iota(jnp.int32, half_count) - half_count
    earlier = sinogram[half_count - 1 : -1]
    middle = sinogram[half_count:]
    following = jnp.concatenate([sinogram[half_count + 1 :], jnp.zeros_like(sinogram[:1])], axis=0)
    chooser = offset[:, None, None]
    partner_rows = jnp.where(chooser < 0, earlier, jnp.where(chooser > 0, following, middle))
    mirrored = jnp.flip(partner_rows, axis=2)
    spread = SPAN
    tile_width = 128
    tile_count = col_count // tile_width
    span_tiles = 2 * spread // tile_width + 1
    window_width = span_tiles * tile_width
    padded = jnp.pad(mirrored, ((0, 0), (0, 0), (spread, spread)))

    def row_profile(row_index):
        leading_row = lax.dynamic_index_in_dim(leading, row_index, 1, False).reshape(
            half_count, tile_count, tile_width
        )
        padded_row = lax.dynamic_index_in_dim(padded, row_index, 1, False).reshape(
            half_count, tile_count + span_tiles - 1, tile_width
        )
        windows = jnp.stack(
            [
                padded_row[:, shift_index : shift_index + tile_count]
                for shift_index in range(span_tiles)
            ],
            axis=2,
        )
        windows = windows.reshape(half_count, tile_count, window_width)
        products = jnp.einsum(
            "iqu,iqv->quv", leading_row, windows, preferred_element_type=jnp.float32
        )
        flattened = jnp.pad(
            products.reshape(tile_count, tile_width * window_width), ((0, 0), (0, tile_width))
        )
        skewed = flattened.reshape(tile_count, tile_width, window_width + 1)[:, :, : 2 * spread]
        return jnp.sum(skewed, axis=(0, 1))

    profile = lax.map(row_profile, lax.iota(jnp.int32, row_share))
    selector = (shifts[None, :] + spread == lax.iota(jnp.int32, 2 * spread)[:, None]).astype(
        jnp.float32
    )
    factor = (half_count * col_count) ** (-0.5)
    correlation = jnp.dot(profile, selector, precision=lax.Precision.HIGHEST) * factor
    return (filtered, correlation)


def solution(mesh):
    in_specs = (
        P(("scan", "ang"), "row", None),
        P("row", None),
        P("row", None),
        P(),
        P("scan"),
        P(),
    )
    out_specs = (P("scan", ("ang", "row"), None), P(("scan", "ang", "row"), None))
    return jax.shard_map(shards, mesh=mesh, in_specs=in_specs, out_specs=out_specs, check_vma=False)
```

profile of v0, /device:TPU:25, one launch (start us, length us, event | category | flops | bytes accessed | tf_op | source)
XLA Modules:
  0.0 509.9 jit_solution(13823215011532389307)
XLA Ops:
  0.6 2.1 fusion.144
  2.7 1.8 fusion.145
  4.5 0.9 convert_element_type.33
  5.4 1.0 convert_subtract_fusion
  6.5 2.2 log_negate_fusion
  8.7 50.3 %multiply_add_fusion = f32[12,32,2560]{2,1,0:T(8,128)S(1)} fusion(f32[12,32,2560]{2,1,0:T(8,128)S(1)} %log_negate_fusion, f32[]{:T(128)} %bitcast.37, f32[]{:T(128)} %bitcast.36, f32[]{:T(128)} %bitcast.35, f32[]{:T(128)} %bitcast.34, f32[]{:T(128)} %bitcast.33, f32[]{:T(128)} %bitcast.32, f32[]{:T(128)} %bitcast.31, f32[]{:T(128)} %bitcast.30, ...), kind=kLoop, calls=%fused_computation.175 | loop fusion | flops 59965440 | bytes 7864444 | tf_op jit(solution)/shard_map/add | solution.py:42
  59.4 1.4 copy-done
  60.8 3.7 collective-permute-start
  64.5 1.9 collective-permute-start.1
  66.4 19.6 %collective-permute-done = f32[12,15,2560]{2,1,0:T(8,128)S(1)} collective-permute-done((f32[12,15,2560]{2,1,0:T(8,128)S(1)}, f32[12,15,2560]{2,1,0:T(8,128)S(1)}, u32[]{:S(2)}, u32[]{:S(2)}) %collective-permute-start) | collective-permute-done | bytes 1843232 | tf_op jit(solution)/shard_map/ppermute | solution.py:19
  86.1 4.5 collective-permute-done.1
  90.6 79.4 %fusion.140 = (f32[12,32]{1,0:T(8,128)S(1)}, f32[12,32,2560]{2,1,0:T(8,128)}) fusion(f32[12,15,2560]{2,1,0:T(8,128)} %collective-permute-done.1, f32[12,32,2560]{2,1,0:T(8,128)} %copy-done, f32[]{:T(128)} %bitcast.37, f32[]{:T(128)} %bitcast.36, f32[]{:T(128)} %bitcast.35, f32[]{:T(128)} %bitcast.34, f32[]{:T(128)} %bitcast.33, f32[]{:T(128)} %bitcast.32, ...), kind=kLoop, calls=%fused_computation.238 | loop fusion | flops 90439296 | bytes 11552380 | tf_op jit(solution)/shard_map/reduce_sum | solution.py:56
  170.0 2.4 fusion.131
  172.6 24.9 %all_to_all.27 = bf16[12,1,4,8,2560]{4,3,0,1,2:T(8,128)(2,1)} all-to-all(bf16[12,1,4,8,2560]{4,3,0,1,2:T(8,128)(2,1)S(1)} %copy.38), channel_id=1, replica_groups=mesh['scan'=2,'ang'=4,'row'=4] {'row'}, dimensions={2} | all-to-all | bytes 3932160 | tf_op jit(solution)/shard_map/all_to_all | solution.py:87
  197.5 4.5 all-to-all-start.1
  202.6 41.5 %all-to-all-done.1 = bf16[12,4,1,8,2560]{4,3,0,2,1:T(8,128)(2,1)S(1)} async-done(((bf16[12,4,1,8,2560]{4,3,0,2,1:T(8,128)(2,1)}), bf16[12,4,1,8,2560]{4,3,0,2,1:T(8,128)(2,1)S(1)}, u32[]{:S(2)}, u32[]{:S(2)}) %all-to-all-start.1) | async-done | bytes 1966112 | tf_op jit(solution)/shard_map/all_to_all | solution.py:88
  244.1 1.3 fusion.143
  245.8 7.4 %rev.4 = bf16[24,8,2560]{2,1,0:T(8,128)(2,1)} reverse(bf16[24,8,2560]{2,1,0:T(8,128)(2,1)S(1)} %slice_select_fusion), dimensions={2} | reverse | bytes 1966080 | tf_op jit(solution)/shard_map/jit(_flip)/rev | solution.py:99
  253.1 1.5 copy.43
  254.6 2.5 copy.40
  257.3 226.5 %while.12 = (s32[]{:T(128)}, f32[8,512]{1,0:T(8,128)S(1)}, s32[8]{0:T(128)S(1)}, bf16[24,8,2560]{2,0,1:T(8,128)(2,1)}, bf16[24,8,3072]{2,0,1:T(8,128)(2,1)S(1)},...) while((s32[]{:T(128)}, f32[8,512]{1,0:T(8,128)S(1)}, s32[8]{0:T(128)S(1)}, bf16[24,8,2560]{2,0,1:T(8,128)(2,1)}, ...), condition=%wide.region_3.4_spmd, body=%wide.region_1.3_spmd.sunk | while | flops 79953408 | bytes 73920672 | solution.py:131
  262.5 1.1 fusion.164
  264.5 4.6 copy.55
  269.0 3.6 pad.485
  272.6 10.1 %reshape.75 = f32[20,128,641]{2,1,0:T(8,128)} reshape(f32[20,82048]{1,0:T(8,128)} %pad.485) | data formatting | bytes 13127680 | tf_op jit(solution)/shard_map/while/body/eval_jaxpr/reshape | solution.py:128
  282.8 2.9 slice_reduce_fusion.2
  290.8 1.1 fusion.164
  292.7 4.6 copy.55
  297.3 3.6 pad.485
  300.9 10.1 %reshape.75 = f32[20,128,641]{2,1,0:T(8,128)} reshape(f32[20,82048]{1,0:T(8,128)} %pad.485) | data formatting | bytes 13127680 | tf_op jit(solution)/shard_map/while/body/eval_jaxpr/reshape | solution.py:128
  311.0 2.9 slice_reduce_fusion.2
  318.0 0.9 constant_dynamic-slice_fusion.2
  319.0 1.1 fusion.164
  321.0 4.6 copy.55
  325.6 3.6 pad.485
  329.1 10.1 %reshape.75 = f32[20,128,641]{2,1,0:T(8,128)} reshape(f32[20,82048]{1,0:T(8,128)} %pad.485) | data formatting | bytes 13127680 | tf_op jit(solution)/shard_map/while/body/eval_jaxpr/reshape | solution.py:128
  339.3 2.9 slice_reduce_fusion.2
  347.3 1.1 fusion.164
  349.3 4.6 copy.55
  353.8 3.6 pad.485
  357.4 10.1 %reshape.75 = f32[20,128,641]{2,1,0:T(8,128)} reshape(f32[20,82048]{1,0:T(8,128)} %pad.485) | data formatting | bytes 13127680 | tf_op jit(solution)/shard_map/while/body/eval_jaxpr/reshape | solution.py:128
  367.5 2.9 slice_reduce_fusion.2
  375.5 1.1 fusion.164
  377.5 4.6 copy.55
  382.1 3.6 pad.485
  385.7 10.1 %reshape.75 = f32[20,128,641]{2,1,0:T(8,128)} reshape(f32[20,82048]{1,0:T(8,128)} %pad.485) | data formatting | bytes 13127680 | tf_op jit(solution)/shard_map/while/body/eval_jaxpr/reshape | solution.py:128
  395.8 2.9 slice_reduce_fusion.2
  402.8 0.9 constant_dynamic-slice_fusion.2
  403.8 1.1 fusion.164
  405.8 4.6 copy.55
  410.3 3.6 pad.485
  413.9 10.1 %reshape.75 = f32[20,128,641]{2,1,0:T(8,128)} reshape(f32[20,82048]{1,0:T(8,128)} %pad.485) | data formatting | bytes 13127680 | tf_op jit(solution)/shard_map/while/body/eval_jaxpr/reshape | solution.py:128
  424.1 2.9 slice_reduce_fusion.2
  432.1 1.1 fusion.164
  434.0 4.6 copy.55
  438.6 3.6 pad.485
  442.2 10.1 %reshape.75 = f32[20,128,641]{2,1,0:T(8,128)} reshape(f32[20,82048]{1,0:T(8,128)} %pad.485) | data formatting | bytes 13127680 | tf_op jit(solution)/shard_map/while/body/eval_jaxpr/reshape | solution.py:128
  452.3 2.9 slice_reduce_fusion.2
  460.3 1.1 fusion.164
  462.3 4.6 copy.55
  466.9 3.6 pad.485
  470.4 10.1 %reshape.75 = f32[20,128,641]{2,1,0:T(8,128)} reshape(f32[20,82048]{1,0:T(8,128)} %pad.485) | data formatting | bytes 13127680 | tf_op jit(solution)/shard_map/while/body/eval_jaxpr/reshape | solution.py:128
  480.6 2.9 slice_reduce_fusion.2
  483.8 25.3 %fusion.130 = bf16[48,8,2560]{2,1,0:T(8,128)(2,1)} fusion(bf16[384,2560]{1,0:T(8,128)(2,1)} %bitcast.121), kind=kOutput, calls=%fused_computation.218 | convolution fusion | flops 5178327040 | bytes 3932160 | tf_op jit(solution)/shard_map/dot_general | solution.py:70
  (130 shorter events, 32.9 us)
Async XLA Ops:
  59.0 1.9 copy-start
  60.8 25.2 %collective-permute-start = (f32[12,15,2560]{2,1,0:T(8,128)S(1)}, f32[12,15,2560]{2,1,0:T(8,128)S(1)}, u32[]{:S(2)}, u32[]{:S(2)}) collective-permute-start(f32[12,15,2560]{2,1,0:T(8,128)S(1)} %get-tuple-element.95), channel_id=1, source_target_pairs={{0,1},{1,2},{2,3},{4,5},{5,6},{6,7},{8,9},{9,10},{10,11},{12,13},{... | collective-permute-start | bytes 5529608 | tf_op jit(solution)/shard_map/ppermute | solution.py:19
  64.5 26.1 %collective-permute-start.1 = (f32[12,15,2560]{2,1,0:T(8,128)S(1)}, f32[12,15,2560]{2,1,0:T(8,128)}, u32[]{:S(2)}, u32[]{:S(2)}) collective-permute-start(f32[12,15,2560]{2,1,0:T(8,128)S(1)} %get-tuple-element.96), channel_id=1, source_target_pairs={{1,0},{2,1},{3,2},{5,4},{6,5},{7,6},{9,8},{10,9},{11,10},{13,12},{... | collective-permute-start | bytes 5529608 | tf_op jit(solution)/shard_map/ppermute | solution.py:21
  172.5 29.5 %copy-start.4 = (s32[24]{0:T(128)S(1)}, s32[24]{0:T(128)}, u32[]{:S(2)}) copy-start(s32[24]{0:T(128)} %param.12) | copy-start | bytes 292
  172.5 29.5 %copy-start.2 = (s32[256]{0:T(256)S(1)}, s32[256]{0:T(256)}, u32[]{:S(2)}) copy-start(s32[256]{0:T(256)} %param.13) | copy-start | bytes 3076
  197.5 46.6 %all-to-all-start.1 = ((bf16[12,4,1,8,2560]{4,3,0,2,1:T(8,128)(2,1)}), bf16[12,4,1,8,2560]{4,3,0,2,1:T(8,128)(2,1)S(1)}, u32[]{:S(2)}, u32[]{:S(2)}) async-start(bf16[12,4,1,8,2560]{4,3,0,2,1:T(8,128)(2,1)} %bitcast.122), calls=%async_computation.1 | async-start | bytes 3932160 | tf_op jit(solution)/shard_map/all_to_all | solution.py:88
  244.1 1.7 copy-start.1
  483.8 25.3 %copy-start.3 = (s32[256]{0:T(256)S(1)}, s32[256]{0:T(256)}, u32[]{:S(2)}) copy-start(s32[256]{0:T(256)} %broadcast_add_fusion) | copy-start | bytes 3076
where the time goes:
time: 517 us; the launch traced here: 510 us
  local copies, waits for them, and re-layouts  197 us (38%)
  other arithmetic  160 us (31%)
  waiting for transfers between devices  65.6 us (13%)
  matrix products  34.6 us (7%)
  blocking collectives  24.9 us (5%)
  loops' own time  16.7 us (3%)
  starting transfers between devices  10.1 us (2%)
    reshape x8, local copies, waits for them, and re-layouts, row_profile(): flattened.reshape(tile_count, tile_width, window_width + 1)  81.2 us
    reduce_sum x1, other arithmetic, center_lines(): jnp.mean(lowpassed, axis=-1, keepdims=True)  79.4 us
    add x1, other arithmetic, column_pass(): summed + kernel_taps[tap_index] * padded[..., tap_index:tap_index + col_c...  50.3 us
    while x64, local copies, waits for them, and re-layouts  45.6 us
    all_to_all x1, waiting for transfers between devices, shards(): lax.all_to_all(across, 'ang', split_axis=1, concat_axis=0, tiled=True)  41.5 us
    pad x8, local copies, waits for them, and re-layouts, row_profile(): jnp.pad(products.reshape(tile_count, tile_width * window_width), ((0, 0),...  28.6 us
    dot_general x1, matrix products, apply_ramp(): jnp.dot(lines.reshape(-1, col_count), ramp_kernel, preferred_element_type...  25.3 us
    all_to_all x1, blocking collectives, shards(): lax.all_to_all(shaped, 'row', split_axis=2, concat_axis=1, tiled=True)  24.9 us
  transfers between devices with their start and end apart: 3, of which 3 were waited for; matrix products, arithmetic and copies ran while one was open for 0% of the time, Pallas kernels for 0%

commit v1 on v0

v1 whole, which is shorter than its diff:
```python
import functools
import math

import jax
import jax.numpy as jnp
from jax import lax
from jax.experimental import pallas as pl
from jax.experimental.pallas import tpu as pltpu
from jax.sharding import PartitionSpec as P

SPAN = 256
LANES = 128
TILE = 256
MESH = pl.DeviceIdType.MESH


def split(value):
    high = value.astype(jnp.bfloat16)
    low = (value - high.astype(jnp.float32)).astype(jnp.bfloat16)
    return high, low


def band(taps_ref, lag, rows_same=None):
    tap_count = taps_ref.shape[0]
    total = jnp.zeros(lag.shape, jnp.float32)
    for tap_index in range(tap_count):
        total = jnp.where(lag == tap_index, taps_ref[tap_index], total)
    if rows_same is not None:
        total = jnp.where(rows_same, total, 0.0)
    return total


def dot(left, right):
    return jnp.dot(left, right, preferred_element_type=jnp.float32)


def filter_kernel(
    sizes,
    taps_ref,
    raw_ref,
    dark_ref,
    flat_ref,
    out_ref,
    halo_ref,
    level_ref,
    dark_ext,
    gain_ext,
    row_band,
    col_high,
    col_low,
    x_high,
    x_low,
    z_high,
    z_low,
    low_ref,
    send_ref,
    level_send,
    level_recv,
    halo_send,
    halo_recv,
    out_send,
    out_recv,
):
    ang_count, row_devices, halo, group = sizes
    planes, rows, cols = raw_ref.shape
    margin = taps_ref.shape[0] // 2
    groups = planes // group
    dests, _, share, _ = send_ref.shape
    ext = rows + 2 * halo
    scan, ang, row = lax.axis_index("scan"), lax.axis_index("ang"), lax.axis_index("row")
    has = (row > 0, row < row_devices - 1)
    peer = (jnp.maximum(row - 1, 0), jnp.minimum(row + 1, row_devices - 1))

    barrier = pltpu.get_barrier_semaphore()
    for a in range(ang_count):
        for b in range(row_devices):

            @pl.when(jnp.logical_or(ang != a, row != b))
            def _():
                pl.semaphore_signal(barrier, inc=1, device_id=(scan, a, b), device_id_type=MESH)

    pl.semaphore_wait(barrier, ang_count * row_devices - 1)

    def level_copy(side, which):
        source = (dark_ref, flat_ref)[which]
        start = 0 if side == 0 else rows - halo
        return pltpu.make_async_remote_copy(
            src_ref=source.at[pl.ds(start, halo)],
            dst_ref=level_ref.at[1 - side, which],
            send_sem=level_send.at[side, which],
            recv_sem=level_recv.at[1 - side, which],
            device_id=(scan, ang, peer[side]),
            device_id_type=MESH,
        )

    def halo_copy(side, g):
        start = 0 if side == 0 else rows - halo
        return pltpu.make_async_remote_copy(
            src_ref=raw_ref.at[pl.ds(g * group, group), pl.ds(start, halo)],
            dst_ref=halo_ref.at[1 - side, pl.ds(g * group, group)],
            send_sem=halo_send.at[side, g],
            recv_sem=halo_recv.at[1 - side, g],
            device_id=(scan, ang, peer[side]),
            device_id_type=MESH,
        )

    def start_halo(g):
        for side in range(2):

            @pl.when(has[side])
            def _():
                halo_copy(side, g).start()

    for side in range(2):

        @pl.when(has[side])
        def _():
            for which in range(2):
                level_copy(side, which).start()

    for g in range(groups):
        start_halo(g)

    out_rows = group * rows
    in_rows = group * ext
    r_out = lax.broadcasted_iota(jnp.int32, (out_rows, in_rows), 0)
    r_in = lax.broadcasted_iota(jnp.int32, (out_rows, in_rows), 1)
    lag = (r_in % ext) - (r_out % rows) - (halo - margin)
    high, low = split(band(taps_ref, lag, r_in // ext == r_out // rows))
    row_band[:out_rows] = high
    row_band[out_rows:] = low
    c_in = lax.broadcasted_iota(jnp.int32, (TILE + 2 * LANES, TILE), 0)
    c_out = lax.broadcasted_iota(jnp.int32, (TILE + 2 * LANES, TILE), 1)
    high, low = split(band(taps_ref, c_in - c_out - (LANES - margin)))
    col_high[...] = high
    col_low[...] = low
    for z_ref in (z_high, z_low):
        z_ref[:, :LANES] = jnp.zeros((out_rows, LANES), jnp.bfloat16)
        z_ref[:, LANES + cols :] = jnp.zeros((out_rows, LANES), jnp.bfloat16)

    def levels(dark, flat):
        dark = dark.astype(jnp.float32)
        return dark, jnp.log(flat.astype(jnp.float32) - dark)

    dark_ext[pl.ds(halo, rows)], gain_ext[pl.ds(halo, rows)] = levels(dark_ref[...], flat_ref[...])
    for side in range(2):

        @pl.when(has[side])
        def _():
            for which in range(2):
                level_copy(1 - side, which).wait_recv()

        at = 0 if side == 0 else halo + rows
        dark_ext[pl.ds(at, halo)], gain_ext[pl.ds(at, halo)] = levels(
            level_ref[side, 0], level_ref[side, 1]
        )

    def target(d):
        index = ang_count * row + d
        return index // row_devices, index % row_devices

    def out_copy(d, g):
        a, b = target(d)
        return pltpu.make_async_remote_copy(
            src_ref=send_ref.at[d, pl.ds(g * group, group)],
            dst_ref=out_ref.at[pl.ds(ang * planes + g * group, group)],
            send_sem=out_send.at[d, g],
            recv_sem=out_recv.at[ang, g],
            device_id=(scan, a, b),
            device_id_type=MESH,
        )

    def own_copy(d, g):
        return pltpu.make_async_copy(
            send_ref.at[d, pl.ds(g * group, group)],
            out_ref.at[pl.ds(ang * planes + g * group, group)],
            out_recv.at[ang, g],
        )

    def is_self(d):
        a, b = target(d)
        return jnp.logical_and(a == ang, b == row)

    for g in range(groups):
        for side in range(2):

            @pl.when(has[side])
            def _():
                halo_copy(1 - side, g).wait_recv()

        def absorb(p, carry):
            plane = g * group + p
            base = pl.multiple_of(p * ext, ext)

            def put(at, counts, valid):
                size = counts.shape[0]
                value = gain_ext[pl.ds(at, size)] - jnp.log(
                    counts.astype(jnp.float32) - dark_ext[pl.ds(at, size)]
                )
                if valid is not None:
                    value = jnp.where(valid, value, 0.0)
                high, low = split(value)
                x_high[pl.ds(base + at, size)] = high
                x_low[pl.ds(base + at, size)] = low

            put(0, halo_ref[0, plane], has[0])
            put(halo, raw_ref[plane], None)
            put(halo + rows, halo_ref[1, plane], has[1])
            return carry

        lax.fori_loop(0, group, absorb, 0)

        def row_pass(n, carry):
            at = pl.multiple_of(n * TILE, TILE)
            both = dot(row_band[...], x_high[:, pl.ds(at, TILE)])
            rest = dot(row_band[:out_rows], x_low[:, pl.ds(at, TILE)])
            high, low = split(both[:out_rows] + (both[out_rows:] + rest))
            to = pl.multiple_of(n * TILE + LANES, LANES)
            z_high[:, pl.ds(to, TILE)] = high
            z_low[:, pl.ds(to, TILE)] = low
            return carry

        lax.fori_loop(0, cols // TILE, row_pass, 0)

        def column_pass(n, total):
            at = pl.multiple_of(n * TILE, TILE)
            window = z_high[:, pl.ds(at, TILE + 2 * LANES)]
            rest = z_low[:, pl.ds(at, TILE + 2 * LANES)]
            value = dot(window, col_high[...]) + (
                dot(window, col_low[...]) + dot(rest, col_high[...])
            )
            low_ref[:, pl.ds(at, TILE)] = value
            return total + jnp.sum(value, axis=1, keepdims=True)

        total = lax.fori_loop(
            0, cols // TILE, column_pass, jnp.zeros((out_rows, 1), jnp.float32)
        )
        mean = total * (1.0 / cols)
        for p in range(group):
            for d in range(dests):
                at = p * rows + d * share
                send_ref[d, g * group + p] = (
                    low_ref[pl.ds(at, share)] - mean[at : at + share]
                ).astype(jnp.bfloat16)
        for d in range(dests):

            @pl.when(is_self(d))
            def _():
                own_copy(d, g).start()

            @pl.when(jnp.logical_not(is_self(d)))
            def _():
                out_copy(d, g).start()

    for g in range(groups):
        for a in range(ang_count):
            place = out_ref.at[pl.ds(a * planes + g * group, group)]
            pltpu.make_async_copy(place, place, out_recv.at[a, g]).wait()
        for d in range(dests):

            @pl.when(jnp.logical_not(is_self(d)))
            def _():
                out_copy(d, g).wait_send()

        for side in range(2):

            @pl.when(has[side])
            def _():
                halo_copy(side, g).wait_send()

    for side in range(2):

        @pl.when(has[side])
        def _():
            for which in range(2):
                level_copy(side, which).wait_send()


def filtered_lines(raw_frames, dark_field, flat_field, kernel_taps):
    planes, rows, cols = raw_frames.shape
    ang_count, row_devices = lax.axis_size("ang"), lax.axis_size("row")
    share = rows // ang_count
    margin = kernel_taps.shape[0] // 2
    halo = -(-margin // 16) * 16
    group = max(g for g in range(1, planes + 1) if planes % g == 0 and g * (rows + 2 * halo) <= 256)
    groups = planes // group
    out_rows, in_rows = group * rows, group * (rows + 2 * halo)
    vmem = pl.BlockSpec(memory_space=pltpu.VMEM)
    bf16, f32 = jnp.bfloat16, jnp.float32
    return pl.pallas_call(
        functools.partial(filter_kernel, (ang_count, row_devices, halo, group)),
        out_shape=jax.ShapeDtypeStruct((ang_count * planes, share, cols), bf16),
        in_specs=[pl.BlockSpec(memory_space=pltpu.SMEM), vmem, vmem, vmem],
        out_specs=pl.BlockSpec(memory_space=pl.ANY),
        scratch_shapes=[
            pltpu.VMEM((2, planes, halo, cols), bf16),
            pltpu.VMEM((2, 2, halo, cols), bf16),
            pltpu.VMEM((rows + 2 * halo, cols), f32),
            pltpu.VMEM((rows + 2 * halo, cols), f32),
            pltpu.VMEM((2 * out_rows, in_rows), bf16),
            pltpu.VMEM((TILE + 2 * LANES, TILE), bf16),
            pltpu.VMEM((TILE + 2 * LANES, TILE), bf16),
            pltpu.VMEM((in_rows, cols), bf16),
            pltpu.VMEM((in_rows, cols), bf16),
            pltpu.VMEM((out_rows, cols + 2 * LANES), bf16),
            pltpu.VMEM((out_rows, cols + 2 * LANES), bf16),
            pltpu.VMEM((out_rows, cols), f32),
            pltpu.VMEM((ang_count, planes, share, cols), bf16),
            pltpu.SemaphoreType.DMA((2, 2)),
            pltpu.SemaphoreType.DMA((2, 2)),
            pltpu.SemaphoreType.DMA((2, groups)),
            pltpu.SemaphoreType.DMA((2, groups)),
            pltpu.SemaphoreType.DMA((ang_count, groups)),
            pltpu.SemaphoreType.DMA((ang_count, groups)),
        ],
        compiler_params=pltpu.CompilerParams(collective_id=0, has_side_effects=True),
    )(kernel_taps, raw_frames, dark_field, flat_field)


def ramp_strip(col_count):
    tiles = col_count // TILE
    shape = ((2 * tiles - 1) * TILE, TILE)
    distance = (
        lax.broadcasted_iota(jnp.int32, shape, 0)
        - lax.broadcasted_iota(jnp.int32, shape, 1)
        - (tiles - 1) * TILE
    )
    spacing = distance.astype(jnp.float32)
    odd_distance = distance % 2 != 0
    falloff = -4.0 / (math.pi * math.pi * jnp.maximum(spacing * spacing, 1.0))
    kernel = jnp.where(distance == 0, 1.0, jnp.where(odd_distance, falloff, 0.0))
    return kernel.astype(jnp.bfloat16)


def ramp_kernel(
    share, partner_ref, shifts_ref, lines_ref, strip_ref, out_ref, corr_ref, x_ref, b_ref, prof_ref
):
    count, cols = lines_ref.shape
    half = count // share // 2
    tiles = cols // TILE
    parts = cols // LANES
    pad = SPAN // LANES
    for q in range(parts):
        x_ref[q] = lines_ref[:, pl.ds(q * LANES, LANES)].astype(jnp.float32)
    for v in range(pad):
        b_ref[v] = jnp.zeros(b_ref.shape[1:], jnp.float32)
        b_ref[pad + parts + v] = jnp.zeros(b_ref.shape[1:], jnp.float32)

    def pick(i, carry):
        source = pl.multiple_of(partner_ref[i] * share, share)
        place = pl.multiple_of(i * share, share)
        b_ref[pl.ds(pad, parts), pl.ds(place, share)] = x_ref[:, pl.ds(source, share)]
        return carry

    lax.fori_loop(0, half, pick, 0)

    def ramp(n, carry):
        start = pl.multiple_of((tiles - 1 - n) * TILE, TILE)
        value = dot(lines_ref[...], strip_ref[pl.ds(start, cols)])
        out_ref[:, pl.ds(pl.multiple_of(n * TILE, TILE), TILE)] = value.astype(jnp.bfloat16)
        return carry

    lax.fori_loop(0, tiles, ramp, 0)

    width = 2 * SPAN + LANES
    for r in range(share):
        rows = pl.ds(r, half, stride=share)
        left = jnp.concatenate(
            [x_ref[q, rows] for q in range(parts)], axis=0
        ).astype(jnp.bfloat16)
        pieces = [b_ref[v, rows] for v in range(parts + 2 * pad)]
        first = parts - 1
        right = jnp.concatenate(
            [
                jnp.concatenate([pieces[first - q + v] for q in range(parts)], axis=0)
                for v in range(width // LANES)
            ],
            axis=1,
        ).astype(jnp.bfloat16)
        product = lax.dot_general(
            left, right, (((0,), (0,)), ((), ())), preferred_element_type=jnp.float32
        )
        skewed = pltpu.roll(product, 0, 1, stride=1, stride_axis=0)
        prof_ref[pl.ds(r, 1)] = jnp.sum(skewed, axis=0, keepdims=True)[:, LANES:]

    lane = lax.broadcasted_iota(jnp.int32, (2 * SPAN, shifts_ref.shape[1]), 0)
    selector = (SPAN - 1 - lane == shifts_ref[...]).astype(jnp.float32)
    corr_ref[...] = jnp.dot(
        prof_ref[...],
        selector,
        precision=lax.Precision.HIGHEST,
        preferred_element_type=jnp.float32,
    ) * ((half * cols) ** -0.5)


def ramp_and_match(lines, partner, shifts):
    count, share, cols = lines.shape
    vmem = pl.BlockSpec(memory_space=pltpu.VMEM)
    half = count // 2
    out, corr = pl.pallas_call(
        functools.partial(ramp_kernel, share),
        out_shape=(
            jax.ShapeDtypeStruct((count * share, cols), jnp.bfloat16),
            jax.ShapeDtypeStruct((share, shifts.shape[0]), jnp.float32),
        ),
        in_specs=[pl.BlockSpec(memory_space=pltpu.SMEM), vmem, vmem, vmem],
        out_specs=(vmem, vmem),
        scratch_shapes=[
            pltpu.VMEM((cols // LANES, count * share, LANES), jnp.float32),
            pltpu.VMEM(((cols + 2 * SPAN) // LANES, half * share, LANES), jnp.float32),
            pltpu.VMEM((share, 2 * SPAN), jnp.float32),
        ],
    )(partner, shifts[None], lines.reshape(count * share, cols), ramp_strip(cols))
    return out.reshape(count, share, cols), corr


def shards(raw_frames, dark_field, flat_field, kernel_taps, partner, shifts):
    lines = filtered_lines(raw_frames, dark_field, flat_field, kernel_taps)
    return ramp_and_match(lines, partner, shifts)


def solution(mesh):
    in_specs = (
        P(("scan", "ang"), "row", None),
        P("row", None),
        P("row", None),
        P(),
        P("scan"),
        P(),
    )
    out_specs = (P("scan", ("ang", "row"), None), P(("scan", "ang", "row"), None))
    return jax.shard_map(shards, mesh=mesh, in_specs=in_specs, out_specs=out_specs, check_vma=False)
```

time: 517 us -> 120 us (0.23)
  the two profiles are of different devices: /device:TPU:25 before, /device:TPU:3 now
where the time goes in v1:
time: 120 us
  Pallas kernels  114 us (95%)
  other arithmetic  5.6 us (5%)
    pallas_call x1, Pallas kernels, filtered_lines(): pl.pallas_call(functools.partial(filter_kernel, (ang_count, row_devices,...  101 us
    pallas_call x1, Pallas kernels, ramp_and_match(): pl.pallas_call(functools.partial(ramp_kernel, share), out_shape=(jax.Shap...  12.5 us
    convert_element_type x1, other arithmetic, ramp_strip(): return kernel.astype(jnp.bfloat16)  5.6 us

profile of v1, /device:TPU:3, one launch (start us, length us, event | category | flops | bytes accessed | tf_op | source)
XLA Modules:
  0.0 120.0 jit_solution(102479632550932128)
XLA Ops:
  0.6 101.2 %shard_map.77 = bf16[48,8,2560]{2,1,0:T(8,128)(2,1)} custom-call(f32[31]{0:T(128)} %taps_ref.1, bf16[12,32,2560]{2,1,0:T(8,128)(2,1)} %raw_ref.1, bf16[32,2560]{1,0:T(8,128)(2,1)} %dark_ref.1, bf16[32,2560]{1,0:T(8,128)(2,1)} %flat_ref.1), custom_call_target="tpu_custom_call" | custom-call | tf_op jit(solution)/shard_map/pallas_call | solution.py:290
  101.8 5.6 %select_convert_fusion.strip_ref = bf16[4864,256]{1,0:T(8,128)(2,1)} fusion(), kind=kLoop, calls=%fused_computation.5 | loop fusion | flops 28639232 | bytes 2490368 | tf_op jit(solution)/shard_map/convert_element_type | solution.py:332
  107.4 12.5 %shard_map.78 = (bf16[384,2560]{1,0:T(8,128)(2,1)}, f32[8,256]{1,0:T(8,128)}) custom-call(s32[24]{0:T(128)} %partner_ref.1, s32[1,256]{1,0:T(1,128)} %bitcast.4, bf16[384,2560]{1,0:T(8,128)(2,1)} %bitcast.3, bf16[4864,256]{1,0:T(8,128)(2,1)} %select_convert_fusion.strip_ref), custom_call_target="tpu_custom_call" | custom-call | tf_op jit(solution)/shard_map/pallas_call | solution.py:400

commit v2 on v1

v2 whole, which is shorter than its diff:
```python
import functools
import math

import jax
import jax.numpy as jnp
from jax import lax
from jax.experimental import pallas as pl
from jax.experimental.pallas import tpu as pltpu
from jax.sharding import PartitionSpec as P

SPAN = 256
LANES = 128
TILE = 256
CORES = 2
MESH = pl.DeviceIdType.MESH


def split(value):
    high = value.astype(jnp.bfloat16)
    low = (value - high.astype(jnp.float32)).astype(jnp.bfloat16)
    return high, low


def band(taps_ref, lag, rows_same=None):
    tap_count = taps_ref.shape[0]
    total = jnp.zeros(lag.shape, jnp.float32)
    for tap_index in range(tap_count):
        total = jnp.where(lag == tap_index, taps_ref[tap_index], total)
    if rows_same is not None:
        total = jnp.where(rows_same, total, 0.0)
    return total


def dot(left, right):
    return jnp.dot(left, right, preferred_element_type=jnp.float32)


def ramp_block(offset):
    shape = (TILE, TILE)
    distance = (
        lax.broadcasted_iota(jnp.int32, shape, 0)
        - lax.broadcasted_iota(jnp.int32, shape, 1)
        + offset
    )
    spacing = distance.astype(jnp.float32)
    odd_distance = (distance & 1) != 0
    falloff = -4.0 / (math.pi * math.pi * jnp.maximum(spacing * spacing, 1.0))
    kernel = jnp.where(distance == 0, 1.0, jnp.where(odd_distance, falloff, 0.0))
    return kernel.astype(jnp.bfloat16)


def unpack(g, planes, group, share, ang_count, lines_ref, x_ref, rows_ref):
    parts = x_ref.shape[0]
    size = group * share
    for a in range(ang_count):
        first = a * planes + g * group
        for p in range(group):
            line = lines_ref[first + p].astype(jnp.float32)
            for q in range(parts):
                x_ref[q, pl.ds((first + p) * share, share)] = line[:, q * LANES : (q + 1) * LANES]
        for q in range(parts):
            rows_ref[pl.ds(a * size, size), pl.ds(q * LANES, LANES)] = x_ref[
                q, pl.ds(first * share, size)
            ].astype(jnp.bfloat16)


def match(share, partner_ref, shifts_ref, corr_ref, x_ref, b_ref, prof_ref):
    parts, count, _ = x_ref.shape
    half = count // share // 2
    cols = parts * LANES
    pad = SPAN // LANES
    for v in range(pad):
        b_ref[v] = jnp.zeros(b_ref.shape[1:], jnp.float32)
        b_ref[pad + parts + v] = jnp.zeros(b_ref.shape[1:], jnp.float32)

    def pick(i, carry):
        offset = partner_ref[i] - i - half
        middle = half + i

        def line(index):
            return x_ref[:, pl.ds(pl.multiple_of(index * share, share), share)]

        following = line(jnp.minimum(middle + 1, 2 * half - 1))
        chosen = jnp.where(offset > 0, following, line(middle))
        place = pl.multiple_of(i * share, share)
        b_ref[pl.ds(pad, parts), pl.ds(place, share)] = jnp.where(
            offset < 0, line(middle - 1), chosen
        )
        return carry

    lax.fori_loop(0, half, pick, 0)
    width = 2 * SPAN + LANES
    for r in range(share):
        rows = pl.ds(r, half, stride=share)
        left = jnp.concatenate(
            [x_ref[q, rows] for q in range(parts)], axis=0
        ).astype(jnp.bfloat16)
        pieces = [b_ref[v, rows] for v in range(parts + 2 * pad)]
        first = parts - 1
        right = jnp.concatenate(
            [
                jnp.concatenate([pieces[first - q + v] for q in range(parts)], axis=0)
                for v in range(width // LANES)
            ],
            axis=1,
        ).astype(jnp.bfloat16)
        product = lax.dot_general(
            left, right, (((0,), (0,)), ((), ())), preferred_element_type=jnp.float32
        )
        skewed = pltpu.roll(product, 0, 1, stride=1, stride_axis=0)
        prof_ref[pl.ds(r, 1)] = jnp.sum(skewed, axis=0, keepdims=True)[:, LANES:]

    lane = lax.broadcasted_iota(jnp.int32, (2 * SPAN, shifts_ref.shape[1]), 0)
    selector = (SPAN - 1 - lane == shifts_ref[...]).astype(jnp.float32)
    corr_ref[...] = jnp.dot(
        prof_ref[...],
        selector,
        precision=lax.Precision.HIGHEST,
        preferred_element_type=jnp.float32,
    ) * ((half * cols) ** -0.5)


def filter_kernel(
    sizes,
    taps_ref,
    raw_ref,
    dark_ref,
    flat_ref,
    partner_ref,
    shifts_ref,
    out_ref,
    corr_ref,
    lines_ref,
    halo_ref,
    level_ref,
    dark_ext,
    gain_ext,
    row_band,
    col_high,
    col_low,
    x_high,
    x_low,
    z_high,
    z_low,
    low_ref,
    send_ref,
    relay_ref,
    strip_ref,
    x_ref,
    rows_ref,
    b_ref,
    prof_ref,
    level_send,
    level_recv,
    halo_send,
    halo_recv,
    out_send,
    out_recv,
    relay_send,
    relay_recv,
):
    ang_count, row_devices, halo, group = sizes
    planes, rows, cols = raw_ref.shape
    margin = taps_ref.shape[0] // 2
    groups = planes // group
    dests, _, share, _ = send_ref.shape
    ext = rows + 2 * halo
    scan, ang, row = lax.axis_index("scan"), lax.axis_index("ang"), lax.axis_index("row")
    has = (row > 0, row < row_devices - 1)
    peer = (jnp.maximum(row - 1, 0), jnp.minimum(row + 1, row_devices - 1))

    barrier = pltpu.get_barrier_semaphore()
    for a in range(ang_count):
        for b in range(row_devices):

            @pl.when(jnp.logical_or(ang != a, row != b))
            def _():
                pl.semaphore_signal(barrier, inc=1, device_id=(scan, a, b), device_id_type=MESH)

    pl.semaphore_wait(barrier, ang_count * row_devices - 1)

    def level_copy(side, which):
        source = (dark_ref, flat_ref)[which]
        start = 0 if side == 0 else rows - halo
        return pltpu.make_async_remote_copy(
            src_ref=source.at[pl.ds(start, halo)],
            dst_ref=level_ref.at[1 - side, which],
            send_sem=level_send.at[side, which],
            recv_sem=level_recv.at[1 - side, which],
            device_id=(scan, ang, peer[side]),
            device_id_type=MESH,
        )

    def halo_copy(side, g):
        start = 0 if side == 0 else rows - halo
        return pltpu.make_async_remote_copy(
            src_ref=raw_ref.at[pl.ds(g * group, group), pl.ds(start, halo)],
            dst_ref=halo_ref.at[1 - side, pl.ds(g * group, group)],
            send_sem=halo_send.at[side, g],
            recv_sem=halo_recv.at[1 - side, g],
            device_id=(scan, ang, peer[side]),
            device_id_type=MESH,
        )

    def start_halo(g):
        for side in range(2):

            @pl.when(has[side])
            def _():
                halo_copy(side, g).start()

    for side in range(2):

        @pl.when(has[side])
        def _():
            for which in range(2):
                level_copy(side, which).start()

    for g in range(groups):
        start_halo(g)

    out_rows = group * rows
    in_rows = group * ext
    r_out = lax.broadcasted_iota(jnp.int32, (out_rows, in_rows), 0)
    r_in = lax.broadcasted_iota(jnp.int32, (out_rows, in_rows), 1)
    lag = (r_in % ext) - (r_out % rows) - (halo - margin)
    high, low = split(band(taps_ref, lag, r_in // ext == r_out // rows))
    row_band[:out_rows] = high
    row_band[out_rows:] = low
    c_in = lax.broadcasted_iota(jnp.int32, (TILE + 2 * LANES, TILE), 0)
    c_out = lax.broadcasted_iota(jnp.int32, (TILE + 2 * LANES, TILE), 1)
    high, low = split(band(taps_ref, c_in - c_out - (LANES - margin)))
    col_high[...] = high
    col_low[...] = low
    for z_ref in (z_high, z_low):
        z_ref[:, :LANES] = jnp.zeros((out_rows, LANES), jnp.bfloat16)
        z_ref[:, LANES + cols :] = jnp.zeros((out_rows, LANES), jnp.bfloat16)

    def levels(dark, flat):
        dark = dark.astype(jnp.float32)
        return dark, jnp.log(flat.astype(jnp.float32) - dark)

    dark_ext[pl.ds(halo, rows)], gain_ext[pl.ds(halo, rows)] = levels(dark_ref[...], flat_ref[...])
    for side in range(2):

        @pl.when(has[side])
        def _():
            for which in range(2):
                level_copy(1 - side, which).wait_recv()

        at = 0 if side == 0 else halo + rows
        dark_ext[pl.ds(at, halo)], gain_ext[pl.ds(at, halo)] = levels(
            level_ref[side, 0], level_ref[side, 1]
        )

    upper = dests // row_devices

    def target(d):
        return upper * row + d // row_devices, d % row_devices

    def is_self(d):
        a, b = target(d)
        return jnp.logical_and(a == ang, b == row)

    def is_relayed(d):
        a, b = target(d)
        return jnp.logical_and(a != ang, b // CORES != row // CORES)

    def part(g):
        return pl.ds(g * group, group)

    def place(a, g):
        return lines_ref.at[pl.ds(a * planes + g * group, group)]

    def out_copy(d, g):
        a, b = target(d)
        return pltpu.make_async_remote_copy(
            src_ref=send_ref.at[d, part(g)],
            dst_ref=place(ang, g),
            send_sem=out_send.at[d, g],
            recv_sem=out_recv.at[ang, g],
            device_id=(scan, a, b),
            device_id_type=MESH,
        )

    def first_hop(d, g):
        return pltpu.make_async_remote_copy(
            src_ref=send_ref.at[d, part(g)],
            dst_ref=relay_ref.at[row, d // row_devices, part(g)],
            send_sem=out_send.at[d, g],
            recv_sem=relay_recv.at[row, d // row_devices, g],
            device_id=(scan, ang, d % row_devices),
            device_id_type=MESH,
        )

    def second_hop(b, u, g):
        return pltpu.make_async_remote_copy(
            src_ref=relay_ref.at[b, u, part(g)],
            dst_ref=place(ang, g),
            send_sem=relay_send.at[b, u, g],
            recv_sem=out_recv.at[ang, g],
            device_id=(scan, upper * b + u, row),
            device_id_type=MESH,
        )

    def own_copy(d, g):
        return pltpu.make_async_copy(send_ref.at[d, part(g)], place(ang, g), out_recv.at[ang, g])

    def relays(b, u):
        return jnp.logical_and(b // CORES != row // CORES, upper * b + u != ang)

    def each_relay(action):
        for b in range(row_devices):
            for u in range(upper):

                @pl.when(relays(b, u))
                def _():
                    action(b, u)

    def relay(g):
        def action(b, u):
            arrived = relay_ref.at[b, u, part(g)]
            pltpu.make_async_copy(arrived, arrived, relay_recv.at[b, u, g]).wait()
            second_hop(b, u, g).start()

        each_relay(action)

    def send(g):
        for d in range(dests):

            @pl.when(is_relayed(d))
            def _():
                first_hop(d, g).start()

        for d in range(dests):

            @pl.when(is_self(d))
            def _():
                own_copy(d, g).start()

            @pl.when(jnp.logical_not(jnp.logical_or(is_relayed(d), is_self(d))))
            def _():
                out_copy(d, g).start()

    for g in range(groups):
        for side in range(2):

            @pl.when(has[side])
            def _():
                halo_copy(1 - side, g).wait_recv()

        def absorb(p, carry):
            plane = g * group + p
            base = pl.multiple_of(p * ext, ext)

            def put(at, counts, valid):
                size = counts.shape[0]
                value = gain_ext[pl.ds(at, size)] - jnp.log(
                    counts.astype(jnp.float32) - dark_ext[pl.ds(at, size)]
                )
                if valid is not None:
                    value = jnp.where(valid, value, 0.0)
                high, low = split(value)
                x_high[pl.ds(base + at, size)] = high
                x_low[pl.ds(base + at, size)] = low

            put(0, halo_ref[0, plane], has[0])
            put(halo, raw_ref[plane], None)
            put(halo + rows, halo_ref[1, plane], has[1])
            return carry

        lax.fori_loop(0, group, absorb, 0)

        def row_pass(n, carry):
            at = pl.multiple_of(n * TILE, TILE)
            both = dot(row_band[...], x_high[:, pl.ds(at, TILE)])
            rest = dot(row_band[:out_rows], x_low[:, pl.ds(at, TILE)])
            high, low = split(both[:out_rows] + (both[out_rows:] + rest))
            to = pl.multiple_of(n * TILE + LANES, LANES)
            z_high[:, pl.ds(to, TILE)] = high
            z_low[:, pl.ds(to, TILE)] = low
            return carry

        lax.fori_loop(0, cols // TILE, row_pass, 0)

        def column_pass(n, total):
            at = pl.multiple_of(n * TILE, TILE)
            window = z_high[:, pl.ds(at, TILE + 2 * LANES)]
            rest = z_low[:, pl.ds(at, TILE + 2 * LANES)]
            value = dot(window, col_high[...]) + (
                dot(window, col_low[...]) + dot(rest, col_high[...])
            )
            low_ref[:, pl.ds(at, TILE)] = value
            return total + jnp.sum(value, axis=1, keepdims=True)

        total = lax.fori_loop(
            0, cols // TILE, column_pass, jnp.zeros((out_rows, 1), jnp.float32)
        )
        mean = total * (1.0 / cols)
        for p in range(group):
            for d in range(dests):
                at = p * rows + d * share
                send_ref[d, g * group + p] = (
                    low_ref[pl.ds(at, share)] - mean[at : at + share]
                ).astype(jnp.bfloat16)
        if g > 0:
            relay(g - 1)
        send(g)

    tiles = cols // TILE

    def build(n, carry):
        base = pl.multiple_of(n * TILE, TILE)
        strip_ref[pl.ds(base, TILE)] = ramp_block(base - (tiles - 1) * TILE)
        return carry

    lax.fori_loop(0, 2 * tiles - 1, build, 0)
    relay(groups - 1)

    size = group * share
    for g in range(groups):
        for a in range(ang_count):
            here = place(a, g)
            pltpu.make_async_copy(here, here, out_recv.at[a, g]).wait()
        unpack(g, planes, group, share, ang_count, lines_ref, x_ref, rows_ref)

        def ramp(n, carry):
            start = pl.multiple_of((tiles - 1 - n) * TILE, TILE)
            value = dot(rows_ref[...], strip_ref[pl.ds(start, cols)])
            at = pl.ds(pl.multiple_of(n * TILE, TILE), TILE)
            for a in range(ang_count):
                for p in range(group):
                    own = a * size + p * share
                    out_ref[a * planes + g * group + p, :, at] = value[own : own + share].astype(
                        jnp.bfloat16
                    )
            return carry

        lax.fori_loop(0, tiles, ramp, 0)

    match(share, partner_ref, shifts_ref, corr_ref, x_ref, b_ref, prof_ref)

    for g in range(groups):
        for d in range(dests):

            @pl.when(jnp.logical_not(is_self(d)))
            def _():
                out_copy(d, g).wait_send()

        each_relay(lambda b, u: second_hop(b, u, g).wait_send())
        for side in range(2):

            @pl.when(has[side])
            def _():
                halo_copy(side, g).wait_send()

    for side in range(2):

        @pl.when(has[side])
        def _():
            for which in range(2):
                level_copy(side, which).wait_send()


def shards(raw_frames, dark_field, flat_field, kernel_taps, partner, shifts):
    planes, rows, cols = raw_frames.shape
    ang_count, row_devices = lax.axis_size("ang"), lax.axis_size("row")
    share = rows // ang_count
    margin = kernel_taps.shape[0] // 2
    halo = -(-margin // 16) * 16
    group = max(g for g in range(1, planes + 1) if planes % g == 0 and g * (rows + 2 * halo) <= 256)
    groups = planes // group
    out_rows, in_rows = group * rows, group * (rows + 2 * halo)
    count, half = ang_count * planes, ang_count * planes // 2
    vmem = pl.BlockSpec(memory_space=pltpu.VMEM)
    smem = pl.BlockSpec(memory_space=pltpu.SMEM)
    bf16, f32 = jnp.bfloat16, jnp.float32
    return pl.pallas_call(
        functools.partial(filter_kernel, (ang_count, row_devices, halo, group)),
        out_shape=(
            jax.ShapeDtypeStruct((count, share, cols), bf16),
            jax.ShapeDtypeStruct((share, shifts.shape[0]), f32),
        ),
        in_specs=[smem, vmem, vmem, vmem, smem, vmem],
        out_specs=(vmem, vmem),
        scratch_shapes=[
            pltpu.VMEM((count, share, cols), bf16),
            pltpu.VMEM((2, planes, halo, cols), bf16),
            pltpu.VMEM((2, 2, halo, cols), bf16),
            pltpu.VMEM((rows + 2 * halo, cols), f32),
            pltpu.VMEM((rows + 2 * halo, cols), f32),
            pltpu.VMEM((2 * out_rows, in_rows), bf16),
            pltpu.VMEM((TILE + 2 * LANES, TILE), bf16),
            pltpu.VMEM((TILE + 2 * LANES, TILE), bf16),
            pltpu.VMEM((in_rows, cols), bf16),
            pltpu.VMEM((in_rows, cols), bf16),
            pltpu.VMEM((out_rows, cols + 2 * LANES), bf16),
            pltpu.VMEM((out_rows, cols + 2 * LANES), bf16),
            pltpu.VMEM((out_rows, cols), f32),
            pltpu.VMEM((ang_count, planes, share, cols), bf16),
            pltpu.VMEM((row_devices, ang_count // row_devices, planes, share, cols), bf16),
            pltpu.VMEM((2 * cols - TILE, TILE), bf16),
            pltpu.VMEM((cols // LANES, count * share, LANES), f32),
            pltpu.VMEM((ang_count * group * share, cols), bf16),
            pltpu.VMEM(((cols + 2 * SPAN) // LANES, half * share, LANES), f32),
            pltpu.VMEM((share, 2 * SPAN), f32),
            pltpu.SemaphoreType.DMA((2, 2)),
            pltpu.SemaphoreType.DMA((2, 2)),
            pltpu.SemaphoreType.DMA((2, groups)),
            pltpu.SemaphoreType.DMA((2, groups)),
            pltpu.SemaphoreType.DMA((ang_count, groups)),
            pltpu.SemaphoreType.DMA((ang_count, groups)),
            pltpu.SemaphoreType.DMA((row_devices, ang_count // row_devices, groups)),
            pltpu.SemaphoreType.DMA((row_devices, ang_count // row_devices, groups)),
        ],
        compiler_params=pltpu.CompilerParams(collective_id=0, has_side_effects=True),
    )(kernel_taps, raw_frames, dark_field, flat_field, partner, shifts[None])


def solution(mesh):
    in_specs = (
        P(("scan", "ang"), "row", None),
        P("row", None),
        P("row", None),
        P(),
        P("scan"),
        P(),
    )
    out_specs = (P("scan", ("ang", "row"), None), P(("scan", "ang", "row"), None))
    return jax.shard_map(shards, mesh=mesh, in_specs=in_specs, out_specs=out_specs, check_vma=False)
```

time: 120 us -> 81.8 us (0.68)
  the two profiles are of different devices: /device:TPU:3 before, /device:TPU:25 now
where the time goes in v2:
time: 81.8 us; the launch traced here: 81.6 us
  Pallas kernels  77.4 us (95%)
  local copies, waits for them, and re-layouts  3.55 us (4%)
    pallas_call x1, Pallas kernels, shards(): pl.pallas_call(functools.partial(filter_kernel, (ang_count, row_devices,...  77.4 us
    unnamed x4, local copies, waits for them, and re-layouts  3.55 us

profile of v2, /device:TPU:25, one launch (start us, length us, event | category | flops | bytes accessed | tf_op | source)
XLA Modules:
  0.0 81.6 jit_solution(18140266011011638692)
XLA Ops:
  0.6 77.4 %shard_map.77 = (bf16[48,8,2560]{2,1,0:T(8,128)(2,1)}, f32[8,256]{1,0:T(8,128)}) custom-call(f32[31]{0:T(128)} %taps_ref.1, bf16[12,32,2560]{2,1,0:T(8,128)(2,1)} %raw_ref.1, bf16[32,2560]{1,0:T(8,128)(2,1)} %dark_ref.1, bf16[32,2560]{1,0:T(8,128)(2,1)} %flat_ref.1, s32[24]{0:T(128)} %partner_ref.1, s32[1,256]{1,0:T(1,128)} %bitcast.1), custom_call_target="tpu_custom_call" | custom-call | tf_op jit(solution)/shard_map/pallas_call | solution.py:478
  78.0 0.0 copy-start
  78.0 2.9 %copy.10 = bf16[48,8,2560]{2,1,0:T(8,128)(2,1)} copy(bf16[48,8,2560]{2,1,0:T(8,128)(2,1)} %get-tuple-element.4) | data formatting | bytes 3932160
  81.0 0.0 copy-done
  81.0 0.6 copy.11
Async XLA Ops:
  78.0 3.0 %copy-start = (f32[8,256]{1,0:T(8,128)S(1)}, f32[8,256]{1,0:T(8,128)}, u32[]{:S(2)}) copy-start(f32[8,256]{1,0:T(8,128)} %get-tuple-element.5) | copy-start | bytes 24580

commit v3 on v2

--- a/solution.py
+++ b/solution.py
@@ -136,8 +136,7 @@
     dark_ext,
     gain_ext,
     row_band,
-    col_high,
-    col_low,
+    col_band,
     x_high,
     x_low,
     z_high,
@@ -159,7 +158,7 @@
     relay_send,
     relay_recv,
 ):
-    ang_count, row_devices, halo, group = sizes
+    ang_count, row_devices, halo, group, joined = sizes
     planes, rows, cols = raw_ref.shape
     margin = taps_ref.shape[0] // 2
     groups = planes // group
@@ -216,7 +215,7 @@
             for which in range(2):
                 level_copy(side, which).start()
 
-    for g in range(groups):
+    for g in range(min(2, groups)):
         start_halo(g)
 
     out_rows = group * rows
@@ -230,8 +229,8 @@
     c_in = lax.broadcasted_iota(jnp.int32, (TILE + 2 * LANES, TILE), 0)
     c_out = lax.broadcasted_iota(jnp.int32, (TILE + 2 * LANES, TILE), 1)
     high, low = split(band(taps_ref, c_in - c_out - (LANES - margin)))
-    col_high[...] = high
-    col_low[...] = low
+    col_band[:, :TILE] = high
+    col_band[:, TILE:] = low
     for z_ref in (z_high, z_low):
         z_ref[:, :LANES] = jnp.zeros((out_rows, LANES), jnp.bfloat16)
         z_ref[:, LANES + cols :] = jnp.zeros((out_rows, LANES), jnp.bfloat16)
@@ -371,31 +370,34 @@
 
         lax.fori_loop(0, group, absorb, 0)
 
+        step = cols // 2 if cols // 2 % TILE == 0 else TILE
+
         def row_pass(n, carry):
-            at = pl.multiple_of(n * TILE, TILE)
-            both = dot(row_band[...], x_high[:, pl.ds(at, TILE)])
-            rest = dot(row_band[:out_rows], x_low[:, pl.ds(at, TILE)])
+            at = pl.multiple_of(n * step, TILE)
+            both = dot(row_band[...], x_high[:, pl.ds(at, step)])
+            rest = dot(row_band[:out_rows], x_low[:, pl.ds(at, step)])
             high, low = split(both[:out_rows] + (both[out_rows:] + rest))
-            to = pl.multiple_of(n * TILE + LANES, LANES)
-            z_high[:, pl.ds(to, TILE)] = high
-            z_low[:, pl.ds(to, TILE)] = low
+            to = pl.multiple_of(n * step + LANES, LANES)
+            z_high[:, pl.ds(to, step)] = high
+            z_low[:, pl.ds(to, step)] = low
             return carry
 
-        lax.fori_loop(0, cols // TILE, row_pass, 0)
-
-        def column_pass(n, total):
-            at = pl.multiple_of(n * TILE, TILE)
-            window = z_high[:, pl.ds(at, TILE + 2 * LANES)]
-            rest = z_low[:, pl.ds(at, TILE + 2 * LANES)]
-            value = dot(window, col_high[...]) + (
-                dot(window, col_low[...]) + dot(rest, col_high[...])
+        lax.fori_loop(0, cols // step, row_pass, 0)
+
+        def windows(z_ref):
+            return jnp.concatenate(
+                [z_ref[:, n * TILE : (n + 1) * TILE + 2 * LANES] for n in range(cols // TILE)],
+                axis=0,
             )
-            low_ref[:, pl.ds(at, TILE)] = value
-            return total + jnp.sum(value, axis=1, keepdims=True)
-
-        total = lax.fori_loop(
-            0, cols // TILE, column_pass, jnp.zeros((out_rows, 1), jnp.float32)
-        )
+
+        both = dot(windows(z_high), col_band[...])
+        rest = dot(windows(z_low), col_band[:, :TILE])
+        value = both[:, :TILE] + (both[:, TILE:] + rest)
+        total = jnp.zeros((out_rows, 1), jnp.float32)
+        for n in range(cols // TILE):
+            tile = value[n * out_rows : (n + 1) * out_rows]
+            low_ref[:, n * TILE : (n + 1) * TILE] = tile
+            total = total + jnp.sum(tile, axis=1, keepdims=True)
         mean = total * (1.0 / cols)
         for p in range(group):
             for d in range(dests):
@@ -406,6 +408,8 @@
         if g > 0:
             relay(g - 1)
         send(g)
+        if g + 2 < groups:
+            start_halo(g + 2)
 
     tiles = cols // TILE
 
@@ -417,21 +421,23 @@
     lax.fori_loop(0, 2 * tiles - 1, build, 0)
     relay(groups - 1)
 
-    size = group * share
-    for g in range(groups):
-        for a in range(ang_count):
-            here = place(a, g)
-            pltpu.make_async_copy(here, here, out_recv.at[a, g]).wait()
-        unpack(g, planes, group, share, ang_count, lines_ref, x_ref, rows_ref)
+    wide = joined * group
+    size = wide * share
+    for h in range(groups // joined):
+        for g in range(h * joined, (h + 1) * joined):
+            for a in range(ang_count):
+                here = place(a, g)
+                pltpu.make_async_copy(here, here, out_recv.at[a, g]).wait()
+        unpack(h, planes, wide, share, ang_count, lines_ref, x_ref, rows_ref)
 
         def ramp(n, carry):
             start = pl.multiple_of((tiles - 1 - n) * TILE, TILE)
             value = dot(rows_ref[...], strip_ref[pl.ds(start, cols)])
             at = pl.ds(pl.multiple_of(n * TILE, TILE), TILE)
             for a in range(ang_count):
-                for p in range(group):
+                for p in range(wide):
                     own = a * size + p * share
-                    out_ref[a * planes + g * group + p, :, at] = value[own : own + share].astype(
+                    out_ref[a * planes + h * wide + p, :, at] = value[own : own + share].astype(
                         jnp.bfloat16
                     )
             return carry
@@ -468,7 +474,8 @@
     share = rows // ang_count
     margin = kernel_taps.shape[0] // 2
     halo = -(-margin // 16) * 16
-    group = max(g for g in range(1, planes + 1) if planes % g == 0 and g * (rows + 2 * halo) <= 256)
+    group = max(g for g in range(1, planes + 1) if planes % g == 0 and g * (rows + 2 * halo) <= 128)
+    joined = 2 if planes // group % 2 == 0 else 1
     groups = planes // group
     out_rows, in_rows = group * rows, group * (rows + 2 * halo)
     count, half = ang_count * planes, ang_count * planes // 2
@@ -476,7 +483,7 @@
     smem = pl.BlockSpec(memory_space=pltpu.SMEM)
     bf16, f32 = jnp.bfloat16, jnp.float32
     return pl.pallas_call(
-        functools.partial(filter_kernel, (ang_count, row_devices, halo, group)),
+        functools.partial(filter_kernel, (ang_count, row_devices, halo, group, joined)),
         out_shape=(
             jax.ShapeDtypeStruct((count, share, cols), bf16),
             jax.ShapeDtypeStruct((share, shifts.shape[0]), f32),
@@ -490,8 +497,7 @@
             pltpu.VMEM((rows + 2 * halo, cols), f32),
             pltpu.VMEM((rows + 2 * halo, cols), f32),
             pltpu.VMEM((2 * out_rows, in_rows), bf16),
-            pltpu.VMEM((TILE + 2 * LANES, TILE), bf16),
-            pltpu.VMEM((TILE + 2 * LANES, TILE), bf16),
+            pltpu.VMEM((TILE + 2 * LANES, 2 * TILE), bf16),
             pltpu.VMEM((in_rows, cols), bf16),
             pltpu.VMEM((in_rows, cols), bf16),
             pltpu.VMEM((out_rows, cols + 2 * LANES), bf16),
@@ -501,7 +507,7 @@
             pltpu.VMEM((row_devices, ang_count // row_devices, planes, share, cols), bf16),
             pltpu.VMEM((2 * cols - TILE, TILE), bf16),
             pltpu.VMEM((cols // LANES, count * share, LANES), f32),
-            pltpu.VMEM((ang_count * group * share, cols), bf16),
+            pltpu.VMEM((ang_count * joined * group * share, cols), bf16),
             pltpu.VMEM(((cols + 2 * SPAN) // LANES, half * share, LANES), f32),
             pltpu.VMEM((share, 2 * SPAN), f32),
             pltpu.SemaphoreType.DMA((2, 2)),

time: 81.8 us -> 73.3 us (0.90)
  Pallas kernels: 77.4 us -> 69 us
    pallas_call x1, Pallas kernels: 77.4 us -> 69 us  [shards(): pl.pallas_call(functools.partial(filter_kernel, (ang_count, row_devices,...]
where the time goes in v3:
time: 73.3 us; the launch traced here: 73.2 us
  Pallas kernels  69 us (94%)
  local copies, waits for them, and re-layouts  3.55 us (5%)
    pallas_call x1, Pallas kernels, shards(): pl.pallas_call(functools.partial(filter_kernel, (ang_count, row_devices,...  69 us
    unnamed x4, local copies, waits for them, and re-layouts  3.55 us

profile of v3, /device:TPU:25, one launch (start us, length us, event | category | flops | bytes accessed | tf_op | source)
XLA Modules:
  0.0 73.2 jit_solution(7731558689719080478)
XLA Ops:
  0.6 69.0 %shard_map.77 = (bf16[48,8,2560]{2,1,0:T(8,128)(2,1)}, f32[8,256]{1,0:T(8,128)}) custom-call(f32[31]{0:T(128)} %taps_ref.1, bf16[12,32,2560]{2,1,0:T(8,128)(2,1)} %raw_ref.1, bf16[32,2560]{1,0:T(8,128)(2,1)} %dark_ref.1, bf16[32,2560]{1,0:T(8,128)(2,1)} %flat_ref.1, s32[24]{0:T(128)} %partner_ref.1, s32[1,256]{1,0:T(1,128)} %bitcast.1), custom_call_target="tpu_custom_call" | custom-call | tf_op jit(solution)/shard_map/pallas_call | solution.py:485
  69.6 0.0 copy-start
  69.6 2.9 %copy.10 = bf16[48,8,2560]{2,1,0:T(8,128)(2,1)} copy(bf16[48,8,2560]{2,1,0:T(8,128)(2,1)} %get-tuple-element.4) | data formatting | bytes 3932160
  72.6 0.0 copy-done
  72.6 0.6 copy.11
Async XLA Ops:
  69.6 3.0 %copy-start = (f32[8,256]{1,0:T(8,128)S(1)}, f32[8,256]{1,0:T(8,128)}, u32[]{:S(2)}) copy-start(f32[8,256]{1,0:T(8,128)} %get-tuple-element.5) | copy-start | bytes 24580
